TPU v7x, 32 devices: a whole 2x2x4 slice. The times are simulated.
32 devices in a mesh: leaf: 4 (over z), row: 2 (over x), top: 4 (over y, core).
Axes of the slice: x: 2, y: 2, z: 4, core: 2. Of those that a mesh axis runs over, the one named last changes fastest.
Arguments:
- loads: bfloat16 [4, 2, 4, 1, 256, 32], P('leaf', 'row', 'top'), may hold values from -6 to 6
- flux_maps: bfloat16 [4, 2, 4, 640, 256], P('leaf', 'row', 'top'), may hold values from -0.375 to 0.375
- chain_maps: float32 [4, 2, 4, 640, 640], P('leaf', 'row', 'top')
- leaf_maps: bfloat16 [4, 2, 4, 1, 256, 256], P('leaf', 'row', 'top'), may hold values from -0.375 to 0.375
- edge_maps: bfloat16 [4, 2, 4, 1, 256, 640], P('leaf', 'row', 'top'), may hold values from -0.25 to 0.25
- top_maps: bfloat16 [4, 2, 4, 1, 256, 128], P('leaf', 'row', 'top'), may hold values from -0.5 to 0.5
- slot_nodes: int32 [4, 2, 4, 128], P('leaf', 'row', 'top'), may hold values from 0 to 8191
- slot_counts: int32 [4, 2, 4], P('leaf', 'row', 'top'), may hold values from 1 to 128, 320 in all within a row
- top_loads: float32 [8192, 32], P('leaf'), may hold values from -6 to 6
- top_inverse: float32 [8192, 8192], P('top', ('leaf', 'row')), may hold values from -0.0625 to 0.0625
Outputs:
- solution: bfloat16 [4, 2, 4, 1, 256, 32], P('leaf', 'row', 'top')
- top_values: float32 [8192, 32], P('top')
Inputs may be any that keep to these rules, and one draw needn't show every extreme that they name: `slot_counts`: over the 4 subtrees of one x-y cell (same x and y, all t) the live slots sum to 320, and one of those subtrees has all 128 slots live.
All inputs are finite; a program needn't handle non-finite values. No bound on the sum of `slot_counts` on one device may be relied on, other than what follows from the above.
Results may differ from a plain program's by a relative error of at most 0.0046.
Values sent between devices are 32-bit elements; how exact they have to be, the bound alone decides.
A program may use at most 64 MiB of HBM per device.

v0:
```python
import jax
import jax.numpy as jnp
from jax import lax
from jax.sharding import PartitionSpec as P


def passed_along(value, axis, steps):
    count = lax.axis_size(axis)
    first, last = (max(0, -steps), min(count, count - steps))
    return lax.ppermute(value, axis, [(source, source + steps) for source in range(first, last)])


def body(
    loads,
    flux_maps,
    chain_maps,
    leaf_maps,
    edge_maps,
    top_maps,
    slot_nodes,
    slot_counts,
    top_loads,
    top_inverse,
):
    leaf_count = loads.shape[3]
    node_count = loads.shape[4]
    rhs_count = loads.shape[5]
    sep_width = chain_maps.shape[-1]
    slot_total = slot_nodes.shape[-1]
    largest_level = lax.Precision.HIGHEST
    local_loads = loads.reshape(leaf_count, node_count, rhs_count)
    flattened = loads.reshape(leaf_count * node_count, rhs_count)
    fluxes = jnp.dot(
        flux_maps.reshape(sep_width, leaf_count * node_count),
        flattened,
        preferred_element_type=jnp.float32,
    )
    combine_operator = chain_maps.reshape(sep_width, sep_width)
    chain_index = lax.axis_index("leaf")

    def advance(step_index, carried):
        earlier = passed_along(carried, "leaf", 1)
        advanced = (
            jnp.dot(
                combine_operator,
                earlier,
                precision=largest_level,
                preferred_element_type=jnp.float32,
            )
            + fluxes
        )
        return jnp.where(chain_index == step_index, advanced, carried)

    states = lax.fori_loop(1, lax.axis_size("leaf"), advance, fluxes)
    slot_ids = slot_nodes.reshape(slot_total)
    is_live = lax.iota(jnp.int32, slot_total) < slot_counts.reshape(())
    chosen_entries = jnp.where(is_live[:, None], states[:slot_total], jnp.float32(0.0))
    block_rows = top_loads.shape[0]
    row_ids = lax.iota(jnp.int32, block_rows * lax.axis_size("leaf"))
    match_table = (row_ids[:, None] == slot_ids[None, :]).astype(jnp.float32)
    top_block = lax.psum_scatter(
        jnp.dot(
            match_table, chosen_entries, precision=largest_level, preferred_element_type=jnp.float32
        ),
        "leaf",
        scatter_dimension=0,
        tiled=True,
    )
    top_block = lax.psum(top_block, ("row", "top"))
    rhs_block = top_loads - top_block
    column_rows = top_inverse.shape[1]
    rhs_piece = lax.dynamic_slice_in_dim(
        rhs_block, lax.axis_index("row") * column_rows, column_rows, 0
    )
    partial_value = jnp.dot(
        top_inverse, rhs_piece, precision=largest_level, preferred_element_type=jnp.float32
    )
    owned_rows = lax.psum(partial_value, ("leaf", "row"))
    shard_piece = lax.all_gather(owned_rows, "top", axis=0, tiled=True)
    row_ids = lax.iota(jnp.int32, shard_piece.shape[0])
    match_table = ((slot_ids[:, None] == row_ids[None, :]) & is_live[:, None]).astype(jnp.float32)
    boundary = jnp.dot(
        match_table, shard_piece, precision=largest_level, preferred_element_type=jnp.float32
    )
    states_low = states.astype(jnp.bfloat16)
    boundary_low = boundary.astype(jnp.bfloat16)
    summed = jnp.einsum(
        "lij,ljr->lir",
        leaf_maps.reshape(leaf_count, node_count, node_count),
        local_loads,
        preferred_element_type=jnp.float32,
    )
    summed = summed + jnp.einsum(
        "lik,kr->lir",
        edge_maps.reshape(leaf_count, node_count, sep_width),
        states_low,
        preferred_element_type=jnp.float32,
    )
    summed = summed + jnp.einsum(
        "lic,cr->lir",
        top_maps.reshape(leaf_count, node_count, slot_total),
        boundary_low,
        preferred_element_type=jnp.float32,
    )
    solution = summed.astype(jnp.bfloat16).reshape(1, 1, 1, leaf_count, node_count, rhs_count)
    return (solution, owned_rows)


def solution(mesh):
    in_specs = (
        P("leaf", "row", "top", None, None, None),
        P("leaf", "row", "top", None, None),
        P("leaf", "row", "top", None, None),
        P("leaf", "row", "top", None, None, None),
        P("leaf", "row", "top", None, None, None),
        P("leaf", "row", "top", None, None, None),
        P("leaf", "row", "top", None),
        P("leaf", "row", "top"),
        P("leaf", None),
        P("top", ("leaf", "row")),
    )
    out_specs = (P("leaf", "row", "top", None, None, None), P("top", None))
    return jax.shard_map(body, mesh=mesh, in_specs=in_specs, out_specs=out_specs, check_vma=False)
```

profile of v0, /device:TPU:0, one launch (start us, length us, event | category | flops | bytes accessed | tf_op | source)
XLA Modules:
  0.0 237.6 jit_solution(16142841711911786712)
XLA Ops:
  7.2 0.0 copy-start
  7.2 0.0 reduce-scatter.2.cloned.1.call-start
  7.9 0.2 copy-done
  8.2 0.9 fusion.15
  9.1 0.0 copy-start.7
  9.1 0.0 copy-start.4
  9.1 29.0 %while.13 = (s32[]{:T(128)}, f32[640,32]{0,1:T(8,128)S(1)}, s32[]{:T(128)}, f32[640,640]{1,0:T(8,128)}, f32[640,32]{0,1:T(8,128)S(1)}, /*index=5*/s32[]{:T(128)}) while((s32[]{:T(128)}, f32[640,32]{0,1:T(8,128)S(1)}, s32[]{:T(128)}, f32[640,640]{1,0:T(8,128)}, f32[640,32]{0,1:T(8,128)S(1)}, /*index=5*/s32[]{:T(128)}) %tuple.44), condition=%wide.region_1.2_spmd, body=%wide.region_0.1_spmd.sunk | while | flops 157327360 | bytes 2293879 | solution.py:54
  9.1 5.1 %collective-permute-start = (f32[640,32]{0,1:T(8,128)S(1)}, f32[640,32]{0,1:T(8,128)S(1)}, u32[]{:S(2)}, u32[]{:S(2)}) collective-permute-start(f32[640,32]{0,1:T(8,128)S(1)} %get-tuple-element.145), channel_id=1, source_target_pairs={{0,8},{8,16},{16,24},{1,9},{9,17},{17,25},{2,10},{10,18},{18,26},{... | collective-permute-start | bytes 245768 | tf_op jit(solution)/shard_map/while/body/eval_jaxpr/ppermute | solution.py:10
  14.2 2.0 collective-permute-done
  16.3 3.1 %fusion.39 = f32[640,32]{0,1:T(8,128)S(1)} fusion(f32[640,32]{0,1:T(8,128)S(1)} %get-tuple-element.145, f32[640,32]{0,1:T(8,128)S(1)} %get-tuple-element.154, f32[640,640]{1,0:T(8,128)} %get-tuple-element.153, f32[640,32]{0,1:T(8,128)S(1)} %collective-permute-done, pred[]{:T(512)S(6)} %eq.69), kind=kOutput, calls=%fused_computation.1.clone.1 | convolution fusion | flops 157327360 | bytes 1966081 | tf_op jit(solution)/shard_map/while/body/eval_jaxpr/dot_general | solution.py:44
  19.4 4.3 %collective-permute-start = (f32[640,32]{0,1:T(8,128)S(1)}, f32[640,32]{0,1:T(8,128)S(1)}, u32[]{:S(2)}, u32[]{:S(2)}) collective-permute-start(f32[640,32]{0,1:T(8,128)S(1)} %get-tuple-element.145), channel_id=1, source_target_pairs={{0,8},{8,16},{16,24},{1,9},{9,17},{17,25},{2,10},{10,18},{18,26},{... | collective-permute-start | bytes 245768 | tf_op jit(solution)/shard_map/while/body/eval_jaxpr/ppermute | solution.py:10
  23.7 2.0 collective-permute-done
  25.7 3.1 %fusion.39 = f32[640,32]{0,1:T(8,128)S(1)} fusion(f32[640,32]{0,1:T(8,128)S(1)} %get-tuple-element.145, f32[640,32]{0,1:T(8,128)S(1)} %get-tuple-element.154, f32[640,640]{1,0:T(8,128)} %get-tuple-element.153, f32[640,32]{0,1:T(8,128)S(1)} %collective-permute-done, pred[]{:T(512)S(6)} %eq.69), kind=kOutput, calls=%fused_computation.1.clone.1 | convolution fusion | flops 157327360 | bytes 1966081 | tf_op jit(solution)/shard_map/while/body/eval_jaxpr/dot_general | solution.py:44
  28.8 4.3 %collective-permute-start = (f32[640,32]{0,1:T(8,128)S(1)}, f32[640,32]{0,1:T(8,128)S(1)}, u32[]{:S(2)}, u32[]{:S(2)}) collective-permute-start(f32[640,32]{0,1:T(8,128)S(1)} %get-tuple-element.145), channel_id=1, source_target_pairs={{0,8},{8,16},{16,24},{1,9},{9,17},{17,25},{2,10},{10,18},{18,26},{... | collective-permute-start | bytes 245768 | tf_op jit(solution)/shard_map/while/body/eval_jaxpr/ppermute | solution.py:10
  33.1 2.0 collective-permute-done
  35.1 3.1 %fusion.39 = f32[640,32]{0,1:T(8,128)S(1)} fusion(f32[640,32]{0,1:T(8,128)S(1)} %get-tuple-element.145, f32[640,32]{0,1:T(8,128)S(1)} %get-tuple-element.154, f32[640,640]{1,0:T(8,128)} %get-tuple-element.153, f32[640,32]{0,1:T(8,128)S(1)} %collective-permute-done, pred[]{:T(512)S(6)} %eq.69), kind=kOutput, calls=%fused_computation.1.clone.1 | convolution fusion | flops 157327360 | bytes 1966081 | tf_op jit(solution)/shard_map/while/body/eval_jaxpr/dot_general | solution.py:44
  38.2 0.0 copy-done.7
  38.2 3.3 %fusion.2 = f32[8192,32]{0,1:T(8,128)} fusion(s32[128]{0:T(128)S(1)} %bitcast.45, f32[640,32]{0,1:T(8,128)S(1)} %get-tuple-element.96, pred[128]{0:T(512)(128)(4,1)S(1)} %iota_compare_fusion.3), kind=kOutput, calls=%fused_computation.5 | convolution fusion | flops 403705856 | bytes 1065984 | tf_op jit(solution)/shard_map/dot_general | solution.py:62
  41.5 0.0 reduce-scatter.2.cloned.1.call-update
  41.5 0.0 all-reduce.3.cloned.1.call-start
  41.6 29.4 %reduce-scatter.2.cloned.1.call-done = f32[2048,32]{0,1:T(8,128)} async-done(((f32[8192,32]{0,1:T(8,128)}), f32[2048,32]{0,1:T(8,128)}) %reduce-scatter.2.cloned.1.call-update) | async-done | bytes 262160 | tf_op jit(solution)/shard_map/reduce_scatter | solution.py:61
  71.0 0.0 all-reduce.3.cloned.1.call-update
  71.0 0.0 all-reduce.5.cloned.1.call-start
  71.1 0.0 copy-start.2
  71.1 0.0 copy-start.3
  71.1 0.0 copy-start.6
  71.1 55.4 %all-reduce.3.cloned.1.call-done = f32[2048,32]{0,1:T(8,128)} async-done(((f32[2048,32]{0,1:T(8,128)}), f32[2048,32]{0,1:T(8,128)}) %all-reduce.3.cloned.1.call-update) | async-done | bytes 262160 | tf_op jit(solution)/shard_map/psum | solution.py:69
  126.5 0.0 copy-done.4
  126.5 11.7 %convolution_bitcast_fusion = f32[2048,32]{0,1:T(8,128)} fusion(f32[2048,1024]{1,0:T(8,128)} %param.21, f32[2048,32]{0,1:T(8,128)} %all-reduce.3.cloned.1.call-done, s32[]{:T(128)S(6)} %select_n.24, f32[2048,32]{0,1:T(8,128)S(1)} %copy-done.4), kind=kOutput, calls=%fused_computation.7 | convolution fusion | flops 805339136 | bytes 8912900 | tf_op jit(solution)/shard_map/dot_general | solution.py:75
  138.2 0.0 copy-start.5
  138.2 0.0 all-reduce.5.cloned.1.call-update
  138.2 0.0 all-gather.2.cloned.1.call-start
  138.2 70.5 %all-reduce.5.cloned.1.call-done = f32[2048,32]{0,1:T(8,128)} async-done(((f32[2048,32]{0,1:T(8,128)}), f32[2048,32]{0,1:T(8,128)}) %all-reduce.5.cloned.1.call-update) | async-done | bytes 262160 | tf_op jit(solution)/shard_map/psum | solution.py:78
  208.7 0.0 copy-start.1
  208.7 0.0 all-gather.2.cloned.1.call-update
  208.8 0.0 copy-done.2
  208.8 0.2 convolution_bitcast_fusion.2
  208.9 0.0 copy-done.3
  209.0 0.0 copy-done.6
  209.0 0.2 convolution_add_fusion.1
  209.2 16.9 %all-gather.2.cloned.1.call-done = f32[8192,32]{0,1:T(8,128)} async-done(((f32[2048,32]{0,1:T(8,128)}), f32[8192,32]{0,1:T(8,128)}) %all-gather.2.cloned.1.call-update) | async-done | bytes 1048592 | tf_op jit(solution)/shard_map/all_gather | solution.py:79
  226.1 3.5 %fusion.8 = bf16[128,32]{1,0:T(8,128)(2,1)S(1)} fusion(f32[8192,32]{0,1:T(8,128)} %all-gather.2.cloned.1.call-done, s32[128]{0:T(128)S(1)} %bitcast.46, pred[128]{0:T(512)(128)(4,1)S(1)} %iota_compare_fusion.3), kind=kOutput, calls=%fused_computation.11 | convolution fusion | flops 404754432 | bytes 1057408 | tf_op jit(solution)/shard_map/dot_general | solution.py:82
  229.6 0.0 copy-done.5
  229.6 0.8 fusion.13
  230.4 0.0 copy-done.1
  230.4 0.7 copy.21
  (2 shorter events, 0.0 us)
Async XLA Ops:
  7.2 1.0 copy-start
  7.2 63.8 %reduce-scatter.2.cloned.1.call-start = ((), (), s32[]{:S(2)}) async-start(), calls=%async_computation.1 | async-start | bytes 1310720 | tf_op jit(solution)/shard_map/reduce_scatter | solution.py:61
  9.1 29.1 %copy-start.7 = (s32[1,1,1,128]{3,2,1,0:T(1,128)S(1)}, s32[1,1,1,128]{3,2,1,0:T(1,128)}, u32[]{:S(2)}) copy-start(s32[1,1,1,128]{3,2,1,0:T(1,128)} %param.18) | copy-start | bytes 1540
  9.1 117.4 %copy-start.4 = (f32[2048,32]{0,1:T(8,128)S(1)}, f32[2048,32]{0,1:T(8,128)}, u32[]{:S(2)}) copy-start(f32[2048,32]{0,1:T(8,128)} %param.20) | copy-start | bytes 786436
  9.1 7.1 %collective-permute-start = (f32[640,32]{0,1:T(8,128)S(1)}, f32[640,32]{0,1:T(8,128)S(1)}, u32[]{:S(2)}, u32[]{:S(2)}) collective-permute-start(f32[640,32]{0,1:T(8,128)S(1)} %get-tuple-element.145), channel_id=1, source_target_pairs={{0,8},{8,16},{16,24},{1,9},{9,17},{17,25},{2,10},{10,18},{18,26},{... | collective-permute-start | bytes 245768 | tf_op jit(solution)/shard_map/while/body/eval_jaxpr/ppermute | solution.py:10
  19.4 6.3 %collective-permute-start = (f32[640,32]{0,1:T(8,128)S(1)}, f32[640,32]{0,1:T(8,128)S(1)}, u32[]{:S(2)}, u32[]{:S(2)}) collective-permute-start(f32[640,32]{0,1:T(8,128)S(1)} %get-tuple-element.145), channel_id=1, source_target_pairs={{0,8},{8,16},{16,24},{1,9},{9,17},{17,25},{2,10},{10,18},{18,26},{... | collective-permute-start | bytes 245768 | tf_op jit(solution)/shard_map/while/body/eval_jaxpr/ppermute | solution.py:10
  28.8 6.3 %collective-permute-start = (f32[640,32]{0,1:T(8,128)S(1)}, f32[640,32]{0,1:T(8,128)S(1)}, u32[]{:S(2)}, u32[]{:S(2)}) collective-permute-start(f32[640,32]{0,1:T(8,128)S(1)} %get-tuple-element.145), channel_id=1, source_target_pairs={{0,8},{8,16},{16,24},{1,9},{9,17},{17,25},{2,10},{10,18},{18,26},{... | collective-permute-start | bytes 245768 | tf_op jit(solution)/shard_map/while/body/eval_jaxpr/ppermute | solution.py:10
  41.5 84.9 %all-reduce.3.cloned.1.call-start = ((), (), s32[]{:S(2)}) async-start(), calls=%async_computation.2 | async-start | bytes 524288 | tf_op jit(solution)/shard_map/psum | solution.py:69
  71.0 137.7 %all-reduce.5.cloned.1.call-start = ((), (), s32[]{:S(2)}) async-start(), calls=%async_computation.3 | async-start | bytes 524288 | tf_op jit(solution)/shard_map/psum | solution.py:78
  71.1 137.7 %copy-start.2 = (bf16[1,1,1,1,256,640]{5,4,3,2,1,0:T(8,128)(2,1)S(1)}, bf16[1,1,1,1,256,640]{5,4,3,2,1,0:T(8,128)(2,1)}, u32[]{:S(2)}) copy-start(bf16[1,1,1,1,256,640]{5,4,3,2,1,0:T(8,128)(2,1)} %param.16) | copy-start | bytes 983044
  71.1 137.9 %copy-start.3 = (bf16[1,1,1,1,256,256]{5,4,3,2,1,0:T(8,128)(2,1)S(1)}, bf16[1,1,1,1,256,256]{5,4,3,2,1,0:T(8,128)(2,1)}, u32[]{:S(2)}) copy-start(bf16[1,1,1,1,256,256]{5,4,3,2,1,0:T(8,128)(2,1)} %param.15) | copy-start | bytes 393220
  71.1 137.9 %copy-start.6 = (bf16[1,1,1,1,256,32]{4,5,3,2,1,0:T(8,128)(2,1)S(1)}, bf16[1,1,1,1,256,32]{4,5,3,2,1,0:T(8,128)(2,1)}, u32[]{:S(2)}) copy-start(bf16[1,1,1,1,256,32]{4,5,3,2,1,0:T(8,128)(2,1)} %param.12) | copy-start | bytes 49156
  138.2 91.4 %copy-start.5 = (bf16[1,1,1,1,256,128]{5,4,3,2,1,0:T(8,128)(2,1)S(1)}, bf16[1,1,1,1,256,128]{5,4,3,2,1,0:T(8,128)(2,1)}, u32[]{:S(2)}) copy-start(bf16[1,1,1,1,256,128]{5,4,3,2,1,0:T(8,128)(2,1)} %param.17) | copy-start | bytes 196612
  138.2 87.9 %all-gather.2.cloned.1.call-start = ((), (), s32[]{:S(2)}) async-start(), calls=%async_computation.4 | async-start | bytes 1310720 | tf_op jit(solution)/shard_map/all_gather | solution.py:79
  208.7 21.6 %copy-start.1 = (f32[2048,32]{0,1:T(8,128)S(1)}, f32[2048,32]{0,1:T(8,128)}, u32[]{:S(2)}) copy-start(f32[2048,32]{0,1:T(8,128)} %all-reduce.5.cloned.1.call-done) | copy-start | bytes 786436
Sparse Core Ops, SparseCore 0:
  41.6 29.3 reduce-scatter.1
  74.1 52.3 all-reduce.2
  138.3 70.3 all-reduce.4
  210.2 15.8 all-gather.1
where the time goes:
time: 238 us
  waiting for transfers between devices  178 us (75%)
  matrix products  29.7 us (12%)
  between operations  14.6 us (6%)
  starting transfers between devices  13.8 us (6%)
    psum x1, waiting for transfers between devices, body(): owned_rows = lax.psum(partial_value, ('leaf', 'row'))  70.5 us
    psum x1, waiting for transfers between devices, body(): top_block = lax.psum(top_block, ('row', 'top'))  55.4 us
    reduce_scatter x1, waiting for transfers between devices, body(): lax.psum_scatter(jnp.dot(match_table, chosen_entries, precision=largest_l...  29.4 us
    all_gather x1, waiting for transfers between devices, body(): shard_piece = lax.all_gather(owned_rows, 'top', axis=0, tiled=True)  16.9 us
    ppermute x3, starting transfers between devices, passed_along(): lax.ppermute(value, axis, [(source, source + steps) for source in range(f...  13.7 us
    dot_general x1, matrix products, body(): jnp.dot(top_inverse, rhs_piece, precision=largest_level, preferred_elemen...  11.7 us
    dot_general x3, matrix products, advance(): jnp.dot(combine_operator, earlier, precision=largest_level, preferred_ele...  9.17 us
    ppermute x3, waiting for transfers between devices, passed_along(): lax.ppermute(value, axis, [(source, source + steps) for source in range(f...  6.09 us
  transfers between devices with their start and end apart: 7, of which 7 were waited for; matrix products, arithmetic and copies ran while one was open for 0% of the time, Pallas kernels for 0%

commit v1 on v0

--- a/solution.py
+++ b/solution.py
@@ -2,6 +2,23 @@
 import jax.numpy as jnp
 from jax import lax
 from jax.sharding import PartitionSpec as P
+
+
+def in_order(parts, dim):
+    parts = jnp.moveaxis(parts, 0, dim)
+    shape = parts.shape
+    return parts.reshape(*shape[:dim], shape[dim] * shape[dim + 1], *shape[dim + 2 :])
+
+
+def gather_around(array, axis, dim):
+    count = lax.axis_size(axis)
+    forward = [(i, (i + 1) % count) for i in range(count)]
+    blocks = [array]
+    while len(blocks) < count:
+        blocks.append(lax.ppermute(blocks[-1], axis, forward))
+    index = lax.axis_index(axis)
+    blocks = jnp.stack(blocks)[(index - jnp.arange(count)) % count]
+    return in_order(blocks, dim)
 
 
 def passed_along(value, axis, steps):
@@ -76,7 +93,7 @@
         top_inverse, rhs_piece, precision=largest_level, preferred_element_type=jnp.float32
     )
     owned_rows = lax.psum(partial_value, ("leaf", "row"))
-    shard_piece = lax.all_gather(owned_rows, "top", axis=0, tiled=True)
+    shard_piece = gather_around(owned_rows, "top", 0)
     row_ids = lax.iota(jnp.int32, shard_piece.shape[0])
     match_table = ((slot_ids[:, None] == row_ids[None, :]) & is_live[:, None]).astype(jnp.float32)
     boundary = jnp.dot(

time: 238 us -> 239 us (level)
    ppermute x0 -> x3, waiting for transfers between devices: none -> 17.2 us  [gather_around(): blocks.append(lax.ppermute(blocks[-1], axis, forward))]
    all_gather x1 -> x0, waiting for transfers between devices: 16.9 us -> none  [body(): shard_piece = lax.all_gather(owned_rows, 'top', axis=0, tiled=True)]
  transfers between devices with their start and end apart: 7 -> 9, of which waited for: 7 -> 9; matrix products, arithmetic and copies ran while one was open for 0% -> 0% of each run, Pallas kernels for 0% -> 0%
where the time goes in v1:
time: 239 us; the launch traced here: 238 us
  waiting for transfers between devices  179 us (75%)
  matrix products  28.4 us (12%)
  between operations  14.6 us (6%)
  starting transfers between devices  13.8 us (6%)
    psum x1, waiting for transfers between devices, body(): owned_rows = lax.psum(partial_value, ('leaf', 'row'))  70.6 us
    psum x1, waiting for transfers between devices, body(): top_block = lax.psum(top_block, ('row', 'top'))  55.4 us
    reduce_scatter x1, waiting for transfers between devices, body(): lax.psum_scatter(jnp.dot(match_table, chosen_entries, precision=largest_l...  29.4 us
    ppermute x3, waiting for transfers between devices, gather_around(): blocks.append(lax.ppermute(blocks[-1], axis, forward))  17.2 us
    ppermute x3, starting transfers between devices, passed_along(): lax.ppermute(value, axis, [(source, source + steps) for source in range(f...  13.7 us
    dot_general x1, matrix products, body(): jnp.dot(top_inverse, rhs_piece, precision=largest_level, preferred_elemen...  11.7 us
    dot_general x3, matrix products, advance(): jnp.dot(combine_operator, earlier, precision=largest_level, preferred_ele...  9.16 us
    ppermute x3, waiting for transfers between devices, passed_along(): lax.ppermute(value, axis, [(source, source + steps) for source in range(f...  6.09 us
  transfers between devices with their start and end apart: 9, of which 9 were waited for; matrix products, arithmetic and copies ran while one was open for 0% of the time, Pallas kernels for 0%

profile of v1, /device:TPU:0, one launch (start us, length us, event | category | flops | bytes accessed | tf_op | source)
XLA Modules:
  0.0 238.4 jit_solution(14037981721983109082)
XLA Ops:
  7.2 0.0 copy-start
  7.2 0.0 reduce-scatter.2.cloned.1.call-start
  7.9 0.2 copy-done
  8.2 0.9 fusion.15
  9.1 0.0 copy-start.7
  9.1 0.0 copy-start.4
  9.1 29.0 %while.13 = (s32[]{:T(128)}, f32[640,32]{0,1:T(8,128)S(1)}, s32[]{:T(128)}, f32[640,640]{1,0:T(8,128)}, f32[640,32]{0,1:T(8,128)S(1)}, /*index=5*/s32[]{:T(128)}) while((s32[]{:T(128)}, f32[640,32]{0,1:T(8,128)S(1)}, s32[]{:T(128)}, f32[640,640]{1,0:T(8,128)}, f32[640,32]{0,1:T(8,128)S(1)}, /*index=5*/s32[]{:T(128)}) %tuple.42), condition=%wide.region_1.2_spmd, body=%wide.region_0.1_spmd.sunk | while | flops 157327360 | bytes 2293879 | solution.py:71
  9.1 5.1 %collective-permute-start = (f32[640,32]{0,1:T(8,128)S(1)}, f32[640,32]{0,1:T(8,128)S(1)}, u32[]{:S(2)}, u32[]{:S(2)}) collective-permute-start(f32[640,32]{0,1:T(8,128)S(1)} %get-tuple-element.145), channel_id=1, source_target_pairs={{0,8},{8,16},{16,24},{1,9},{9,17},{17,25},{2,10},{10,18},{18,26},{... | collective-permute-start | bytes 245768 | tf_op jit(solution)/shard_map/while/body/eval_jaxpr/ppermute | solution.py:27
  14.2 2.0 collective-permute-done
  16.3 3.1 %fusion.41 = f32[640,32]{0,1:T(8,128)S(1)} fusion(f32[640,32]{0,1:T(8,128)S(1)} %get-tuple-element.145, f32[640,32]{0,1:T(8,128)S(1)} %get-tuple-element.154, f32[640,640]{1,0:T(8,128)} %get-tuple-element.153, f32[640,32]{0,1:T(8,128)S(1)} %collective-permute-done, pred[]{:T(512)S(6)} %eq.71), kind=kOutput, calls=%fused_computation.2.clone.1 | convolution fusion | flops 157327360 | bytes 1966081 | tf_op jit(solution)/shard_map/while/body/eval_jaxpr/dot_general | solution.py:61
  19.4 4.3 %collective-permute-start = (f32[640,32]{0,1:T(8,128)S(1)}, f32[640,32]{0,1:T(8,128)S(1)}, u32[]{:S(2)}, u32[]{:S(2)}) collective-permute-start(f32[640,32]{0,1:T(8,128)S(1)} %get-tuple-element.145), channel_id=1, source_target_pairs={{0,8},{8,16},{16,24},{1,9},{9,17},{17,25},{2,10},{10,18},{18,26},{... | collective-permute-start | bytes 245768 | tf_op jit(solution)/shard_map/while/body/eval_jaxpr/ppermute | solution.py:27
  23.7 2.0 collective-permute-done
  25.7 3.1 %fusion.41 = f32[640,32]{0,1:T(8,128)S(1)} fusion(f32[640,32]{0,1:T(8,128)S(1)} %get-tuple-element.145, f32[640,32]{0,1:T(8,128)S(1)} %get-tuple-element.154, f32[640,640]{1,0:T(8,128)} %get-tuple-element.153, f32[640,32]{0,1:T(8,128)S(1)} %collective-permute-done, pred[]{:T(512)S(6)} %eq.71), kind=kOutput, calls=%fused_computation.2.clone.1 | convolution fusion | flops 157327360 | bytes 1966081 | tf_op jit(solution)/shard_map/while/body/eval_jaxpr/dot_general | solution.py:61
  28.8 4.3 %collective-permute-start = (f32[640,32]{0,1:T(8,128)S(1)}, f32[640,32]{0,1:T(8,128)S(1)}, u32[]{:S(2)}, u32[]{:S(2)}) collective-permute-start(f32[640,32]{0,1:T(8,128)S(1)} %get-tuple-element.145), channel_id=1, source_target_pairs={{0,8},{8,16},{16,24},{1,9},{9,17},{17,25},{2,10},{10,18},{18,26},{... | collective-permute-start | bytes 245768 | tf_op jit(solution)/shard_map/while/body/eval_jaxpr/ppermute | solution.py:27
  33.1 2.0 collective-permute-done
  35.1 3.1 %fusion.41 = f32[640,32]{0,1:T(8,128)S(1)} fusion(f32[640,32]{0,1:T(8,128)S(1)} %get-tuple-element.145, f32[640,32]{0,1:T(8,128)S(1)} %get-tuple-element.154, f32[640,640]{1,0:T(8,128)} %get-tuple-element.153, f32[640,32]{0,1:T(8,128)S(1)} %collective-permute-done, pred[]{:T(512)S(6)} %eq.71), kind=kOutput, calls=%fused_computation.2.clone.1 | convolution fusion | flops 157327360 | bytes 1966081 | tf_op jit(solution)/shard_map/while/body/eval_jaxpr/dot_general | solution.py:61
  38.2 0.0 copy-done.7
  38.2 3.3 %fusion.2 = f32[8192,32]{0,1:T(8,128)} fusion(s32[128]{0:T(128)S(1)} %bitcast.59, f32[640,32]{0,1:T(8,128)S(1)} %get-tuple-element.96, pred[128]{0:T(512)(128)(4,1)S(1)} %iota_compare_fusion.3), kind=kOutput, calls=%fused_computation.6 | convolution fusion | flops 403705856 | bytes 1065984 | tf_op jit(solution)/shard_map/dot_general | solution.py:79
  41.5 0.0 reduce-scatter.2.cloned.1.call-update
  41.5 0.0 all-reduce.3.cloned.1.call-start
  41.6 29.4 %reduce-scatter.2.cloned.1.call-done = f32[2048,32]{0,1:T(8,128)} async-done(((f32[8192,32]{0,1:T(8,128)}), f32[2048,32]{0,1:T(8,128)}) %reduce-scatter.2.cloned.1.call-update) | async-done | bytes 262160 | tf_op jit(solution)/shard_map/reduce_scatter | solution.py:78
  71.0 0.0 all-reduce.3.cloned.1.call-update
  71.0 0.0 all-reduce.5.cloned.1.call-start
  71.1 0.0 copy-start.2
  71.1 0.0 copy-start.3
  71.1 0.0 copy-start.6
  71.1 55.4 %all-reduce.3.cloned.1.call-done = f32[2048,32]{0,1:T(8,128)} async-done(((f32[2048,32]{0,1:T(8,128)}), f32[2048,32]{0,1:T(8,128)}) %all-reduce.3.cloned.1.call-update) | async-done | bytes 262160 | tf_op jit(solution)/shard_map/psum | solution.py:86
  126.5 0.0 copy-done.4
  126.5 11.7 %convolution_bitcast_fusion = f32[2048,32]{0,1:T(8,128)} fusion(f32[2048,1024]{1,0:T(8,128)} %param.21, f32[2048,32]{0,1:T(8,128)} %all-reduce.3.cloned.1.call-done, s32[]{:T(128)S(6)} %select_n.48, f32[2048,32]{0,1:T(8,128)S(1)} %copy-done.4), kind=kOutput, calls=%fused_computation.8 | convolution fusion | flops 805339136 | bytes 8912900 | tf_op jit(solution)/shard_map/dot_general | solution.py:92
  138.1 0.0 all-reduce.5.cloned.1.call-update
  138.2 70.6 %all-reduce.5.cloned.1.call-done = f32[2048,32]{0,1:T(8,128)} async-done(((f32[2048,32]{0,1:T(8,128)}), f32[2048,32]{0,1:T(8,128)}) %all-reduce.5.cloned.1.call-update) | async-done | bytes 262160 | tf_op jit(solution)/shard_map/psum | solution.py:95
  208.7 0.0 collective-permute-start.1
  208.7 6.0 %collective-permute-done.1 = f32[2048,32]{0,1:T(8,128)S(1)} collective-permute-done((f32[2048,32]{0,1:T(8,128)}, f32[2048,32]{0,1:T(8,128)S(1)}, u32[]{:S(2)}, u32[]{:S(2)}) %collective-permute-start.1) | collective-permute-done | bytes 262176 | tf_op jit(solution)/shard_map/ppermute | solution.py:18
  214.7 0.0 collective-permute-start.2
  214.7 0.0 copy-done.2
  214.8 0.2 convolution_bitcast_fusion.2
  214.9 5.6 %collective-permute-done.2 = f32[2048,32]{0,1:T(8,128)S(1)} collective-permute-done((f32[2048,32]{0,1:T(8,128)S(1)}, f32[2048,32]{0,1:T(8,128)S(1)}, u32[]{:S(2)}, u32[]{:S(2)}) %collective-permute-start.2) | collective-permute-done | bytes 262176 | tf_op jit(solution)/shard_map/ppermute | solution.py:18
  220.5 0.0 collective-permute-start.3
  220.5 0.0 copy-done.3
  220.5 0.0 copy-done.6
  220.6 0.2 convolution_add_fusion.1
  220.7 5.6 %collective-permute-done.3 = f32[2048,32]{0,1:T(8,128)S(1)} collective-permute-done((f32[2048,32]{0,1:T(8,128)S(1)}, f32[2048,32]{0,1:T(8,128)S(1)}, u32[]{:S(2)}, u32[]{:S(2)}) %collective-permute-start.3) | collective-permute-done | bytes 262176 | tf_op jit(solution)/shard_map/ppermute | solution.py:18
  226.3 1.0 pad_maximum_fusion
  227.3 0.6 gather_fusion
  228.0 0.0 copy-start.5
  228.0 0.0 copy-start.1
  228.0 0.1 copy.13
  228.1 2.3 fusion.8
  230.3 0.0 copy-done.5
  230.3 0.8 fusion.13
  231.1 0.0 copy-done.1
  231.1 0.7 copy.23
  (4 shorter events, 0.1 us)
Async XLA Ops:
  7.2 1.0 copy-start
  7.2 63.8 %reduce-scatter.2.cloned.1.call-start = ((), (), s32[]{:S(2)}) async-start(), calls=%async_computation.1 | async-start | bytes 1310720 | tf_op jit(solution)/shard_map/reduce_scatter | solution.py:78
  9.1 29.1 %copy-start.7 = (s32[1,1,1,128]{3,2,1,0:T(1,128)S(1)}, s32[1,1,1,128]{3,2,1,0:T(1,128)}, u32[]{:S(2)}) copy-start(s32[1,1,1,128]{3,2,1,0:T(1,128)} %param.18) | copy-start | bytes 1540
  9.1 117.3 %copy-start.4 = (f32[2048,32]{0,1:T(8,128)S(1)}, f32[2048,32]{0,1:T(8,128)}, u32[]{:S(2)}) copy-start(f32[2048,32]{0,1:T(8,128)} %param.20) | copy-start | bytes 786436
  9.1 7.1 %collective-permute-start = (f32[640,32]{0,1:T(8,128)S(1)}, f32[640,32]{0,1:T(8,128)S(1)}, u32[]{:S(2)}, u32[]{:S(2)}) collective-permute-start(f32[640,32]{0,1:T(8,128)S(1)} %get-tuple-element.145), channel_id=1, source_target_pairs={{0,8},{8,16},{16,24},{1,9},{9,17},{17,25},{2,10},{10,18},{18,26},{... | collective-permute-start | bytes 245768 | tf_op jit(solution)/shard_map/while/body/eval_jaxpr/ppermute | solution.py:27
  19.4 6.3 %collective-permute-start = (f32[640,32]{0,1:T(8,128)S(1)}, f32[640,32]{0,1:T(8,128)S(1)}, u32[]{:S(2)}, u32[]{:S(2)}) collective-permute-start(f32[640,32]{0,1:T(8,128)S(1)} %get-tuple-element.145), channel_id=1, source_target_pairs={{0,8},{8,16},{16,24},{1,9},{9,17},{17,25},{2,10},{10,18},{18,26},{... | collective-permute-start | bytes 245768 | tf_op jit(solution)/shard_map/while/body/eval_jaxpr/ppermute | solution.py:27
  28.8 6.3 %collective-permute-start = (f32[640,32]{0,1:T(8,128)S(1)}, f32[640,32]{0,1:T(8,128)S(1)}, u32[]{:S(2)}, u32[]{:S(2)}) collective-permute-start(f32[640,32]{0,1:T(8,128)S(1)} %get-tuple-element.145), channel_id=1, source_target_pairs={{0,8},{8,16},{16,24},{1,9},{9,17},{17,25},{2,10},{10,18},{18,26},{... | collective-permute-start | bytes 245768 | tf_op jit(solution)/shard_map/while/body/eval_jaxpr/ppermute | solution.py:27
  41.5 84.9 %all-reduce.3.cloned.1.call-start = ((), (), s32[]{:S(2)}) async-start(), calls=%async_computation.2 | async-start | bytes 524288 | tf_op jit(solution)/shard_map/psum | solution.py:86
  71.0 137.7 %all-reduce.5.cloned.1.call-start = ((), (), s32[]{:S(2)}) async-start(), calls=%async_computation.3 | async-start | bytes 524288 | tf_op jit(solution)/shard_map/psum | solution.py:95
  71.1 143.7 %copy-start.2 = (bf16[1,1,1,1,256,640]{5,4,3,2,1,0:T(8,128)(2,1)S(1)}, bf16[1,1,1,1,256,640]{5,4,3,2,1,0:T(8,128)(2,1)}, u32[]{:S(2)}) copy-start(bf16[1,1,1,1,256,640]{5,4,3,2,1,0:T(8,128)(2,1)} %param.16) | copy-start | bytes 983044
  71.1 149.5 %copy-start.3 = (bf16[1,1,1,1,256,256]{5,4,3,2,1,0:T(8,128)(2,1)S(1)}, bf16[1,1,1,1,256,256]{5,4,3,2,1,0:T(8,128)(2,1)}, u32[]{:S(2)}) copy-start(bf16[1,1,1,1,256,256]{5,4,3,2,1,0:T(8,128)(2,1)} %param.15) | copy-start | bytes 393220
  71.1 149.5 %copy-start.6 = (bf16[1,1,1,1,256,32]{4,5,3,2,1,0:T(8,128)(2,1)S(1)}, bf16[1,1,1,1,256,32]{4,5,3,2,1,0:T(8,128)(2,1)}, u32[]{:S(2)}) copy-start(bf16[1,1,1,1,256,32]{4,5,3,2,1,0:T(8,128)(2,1)} %param.12) | copy-start | bytes 49156
  208.7 6.0 %collective-permute-start.1 = (f32[2048,32]{0,1:T(8,128)}, f32[2048,32]{0,1:T(8,128)S(1)}, u32[]{:S(2)}, u32[]{:S(2)}) collective-permute-start(f32[2048,32]{0,1:T(8,128)} %all-reduce.5.cloned.1.call-done), channel_id=1, source_target_pairs={{0,1},{1,2},{2,3},{3,0},{4,5},{5,6},{6,7},{7,4},{8,9},{9,10},{10,1... | collective-permute-start | bytes 786440 | tf_op jit(solution)/shard_map/ppermute | solution.py:18
  214.7 5.8 %collective-permute-start.2 = (f32[2048,32]{0,1:T(8,128)S(1)}, f32[2048,32]{0,1:T(8,128)S(1)}, u32[]{:S(2)}, u32[]{:S(2)}) collective-permute-start(f32[2048,32]{0,1:T(8,128)S(1)} %collective-permute-done.1), channel_id=1, source_target_pairs={{0,1},{1,2},{2,3},{3,0},{4,5},{5,6},{6,7},{7,4},{8,9},{9,10},{10,1... | collective-permute-start | bytes 786440 | tf_op jit(solution)/shard_map/ppermute | solution.py:18
  220.5 5.8 %collective-permute-start.3 = (f32[2048,32]{0,1:T(8,128)S(1)}, f32[2048,32]{0,1:T(8,128)S(1)}, u32[]{:S(2)}, u32[]{:S(2)}) collective-permute-start(f32[2048,32]{0,1:T(8,128)S(1)} %collective-permute-done.2), channel_id=1, source_target_pairs={{0,1},{1,2},{2,3},{3,0},{4,5},{5,6},{6,7},{7,4},{8,9},{9,10},{10,1... | collective-permute-start | bytes 786440 | tf_op jit(solution)/shard_map/ppermute | solution.py:18
  228.0 2.4 copy-start.5
  228.0 3.1 %copy-start.1 = (f32[2048,32]{0,1:T(8,128)S(1)}, f32[2048,32]{0,1:T(8,128)}, u32[]{:S(2)}) copy-start(f32[2048,32]{0,1:T(8,128)} %all-reduce.5.cloned.1.call-done) | copy-start | bytes 786436
Sparse Core Ops, SparseCore 0:
  41.6 29.3 reduce-scatter.1
  74.0 52.3 all-reduce.2
  138.3 70.3 all-reduce.4
